TPU v7x, 256 devices: a whole 4x4x8 slice. The times are simulated.
256 devices in a mesh: mesh: 64 (over x, z, core), sub: 4 (over y).
Axes of the slice: x: 4, y: 4, z: 8, core: 2. Of those that a mesh axis runs over, the one named last changes fastest.
Arguments:
- coords: float32 [3, 524288], P(None, ('mesh', 'sub')), may hold values from -6 to 6
- veloc: float32 [3, 524288], P(None, ('mesh', 'sub')), may hold values from -6 to 6
- node_mass: float32 [524288], P(('mesh', 'sub')), may hold values from 0.5 to 2
- stress: float32 [3, 1048576], P(None, ('mesh', 'sub')), may hold values from -4 to 4
- connect: int32 [4, 1048576], P(None, ('mesh', 'sub')), may hold values from 0 to 3071
- send_mesh: int32 [131072], P(('mesh', 'sub')), may hold values from 0 to 2047
- send_sub: int32 [131072], P(('mesh', 'sub')), may hold values from 0 to 2047
- send_pick: int32 [4, 32768], P(None, ('mesh', 'sub')), may hold values from 0 to 31
- bucket_list: int32 [4, 4, 4096], P(None, None, ('mesh', 'sub')), may hold values from 0 to 127
- pair_mask: int32 [4, 4, 524288], P(None, None, ('mesh', 'sub')), may hold values 0 or 1
Outputs:
- veloc_out: float32 [3, 524288], P(None, ('mesh', 'sub'))
- stress_out: float32 [3, 1048576], P(None, ('mesh', 'sub'))
Inputs may be any that keep to these rules, and one draw needn't show every extreme that they name: `connect`: columns below 2048 are own nodes, then 512 mesh ghosts, then 512 sub ghosts. `send_pick`: a block may be sent to several receivers and several places.
All inputs are finite; a program needn't handle non-finite values. No bound on the sum of `pair_mask` on one device may be relied on, other than what follows from the above.
Results may differ from a plain program's by a relative error of at most 0.0003.
Values sent between devices are 32-bit elements; how exact they have to be, the bound alone decides.
A program may use at most 64 MiB of HBM per device.

v0:
```python
import functools
import math

import jax
import jax.numpy as jnp
from jax import lax
from jax.experimental import pallas as pl
from jax.experimental.pallas import tpu as pltpu
from jax.sharding import PartitionSpec as P

SEG = 128
STEPS = 4
CAP = 2
TIME_STEP = 0.2
YOUNG = 1.0
POISSON = 0.3
HOURGLASS = 0.01
PENALTY = 0.2
REACH = 4.0
PLANE_STIFF = YOUNG / (1.0 - POISSON * POISSON)
SHEAR_STIFF = YOUNG / (2.0 * (1.0 + POISSON))
EXP2_SCALE = math.log2(math.e) / REACH
MESH = pl.DeviceIdType.MESH
F32 = jnp.float32
BF16 = jnp.bfloat16
NT = (((1,), (1,)), ((), ()))
GHOST_ROWS = 4


def dot_nt(lhs, rhs):
    return lax.dot_general(lhs, rhs, NT, preferred_element_type=F32)


def halves(value):
    top = value.astype(BF16)
    return top, (value - top.astype(F32)).astype(BF16)


def cross(u, v):
    return (
        u[1] * v[2] - u[2] * v[1],
        u[2] * v[0] - u[0] * v[2],
        u[0] * v[1] - u[1] * v[0],
    )


def dot3(u, v):
    return u[0] * v[0] + u[1] * v[1] + u[2] * v[2]


def kernel(
    own_rows,
    blocks,
    cands,
    coords,
    veloc,
    mass_in,
    stress_in,
    connect,
    send_mesh,
    send_sub,
    picks,
    buckets,
    pick_lanes,
    bucket_lanes,
    pair_mask,
    vel_out,
    stress_out,
    ids,
    sids,
    pos,
    vel,
    mass,
    cpos,
    cvel,
    snow,
    nrm,
    area,
    geo,
    send_geo,
    recv_geo,
    onehot,
    onehot_back,
    spread,
    fint,
    table,
    pcol,
    mcol,
    wtop,
    wlow,
    wsum,
    slave,
    ret_send,
    ret_recv,
    p_send_m,
    p_send_s,
    p_recv_m,
    p_recv_s,
    v_send_m,
    v_send_s,
    v_recv_m,
    v_recv_s,
    f_send_m,
    f_send_s,
    f_recv_m,
    f_recv_s,
    halo_sem,
    geo_sem,
    ret_sem,
):
    peers = lax.axis_size("mesh")
    subs = lax.axis_size("sub")
    me = lax.axis_index("mesh")
    my_sub = lax.axis_index("sub")
    mesh_next = (lax.rem(me + 1, peers), my_sub)
    mesh_prev = (lax.rem(me + peers - 1, peers), my_sub)
    sub_next = (me, lax.rem(my_sub + 1, subs))
    sub_prev = (me, lax.rem(my_sub + subs - 1, subs))
    slots = peers * CAP
    chunks = blocks // 8
    pairs = cands * own_rows

    barrier = pltpu.get_barrier_semaphore()

    def greet(hop, carry):
        pl.semaphore_signal(
            barrier, inc=1, device_id=(lax.rem(me + hop, peers), my_sub), device_id_type=MESH
        )
        return carry

    lax.fori_loop(1, peers, greet, 0)
    for other in (sub_next, sub_prev):
        pl.semaphore_signal(barrier, inc=1, device_id=other, device_id_type=MESH)

    def lanes_of(row):
        return pl.ds(pl.multiple_of(row * SEG, SEG), SEG)

    def rows_of_nodes(row, carry):
        for c in range(3):
            pos[c, pl.ds(row, 1), :] = coords[pl.ds(c, 1), lanes_of(row)]
            vel[c, pl.ds(row, 1), :] = veloc[pl.ds(c, 1), lanes_of(row)]
        mass[pl.ds(row, 1), :] = mass_in[:, lanes_of(row)]
        return carry

    def rows_of_elems(row, carry):
        for c in range(3):
            snow[c, pl.ds(row, 1), :] = stress_in[pl.ds(c, 1), lanes_of(row)]
        for i in range(4):
            ids[i, pl.ds(row, 1), :] = connect[pl.ds(i, 1), lanes_of(row)]
        return carry

    lax.fori_loop(0, own_rows, rows_of_nodes, 0)
    for r in range(GHOST_ROWS):
        sids[r : r + 1, :] = send_mesh[:, r * SEG : (r + 1) * SEG]
        sids[GHOST_ROWS + r : GHOST_ROWS + r + 1, :] = send_sub[:, r * SEG : (r + 1) * SEG]

    def take(tables, rows, index):
        low = lax.bitwise_and(index, SEG - 1)
        high = lax.shift_right_logical(index, 7)
        found = [jnp.zeros(index.shape, F32) for _ in range(3)]
        for r in range(rows):
            here = high == r
            for c in range(3):
                source = jnp.broadcast_to(tables[c, r : r + 1, :], index.shape)
                got = jnp.take_along_axis(source, low, axis=1, mode="promise_in_bounds")
                found[c] = jnp.where(here, got, found[c])
        return found

    def halo_copy(src, dst, slot, target):
        return pltpu.make_async_remote_copy(
            src_ref=src,
            dst_ref=dst,
            send_sem=halo_sem.at[slot],
            recv_sem=halo_sem.at[slot + 1],
            device_id=target,
            device_id_type=MESH,
        )

    def velocity_copies(step):
        base = 4 + step * 8
        return (
            halo_copy(v_send_m.at[step], v_recv_m.at[step], base, mesh_next),
            halo_copy(v_send_s.at[step], v_recv_s.at[step], base + 2, sub_next),
        )

    def force_copies(step):
        base = 4 + step * 8 + 4
        return (
            halo_copy(f_send_m.at[step], f_recv_m.at[step], base, mesh_prev),
            halo_copy(f_send_s.at[step], f_recv_s.at[step], base + 2, sub_prev),
        )

    position_copies = (
        halo_copy(p_send_m, p_recv_m, 0, mesh_next),
        halo_copy(p_send_s, p_recv_s, 2, sub_next),
    )

    def stage_velocity(step):
        got = take(vel, own_rows, sids[...])
        for c in range(3):
            v_send_m[step, c] = got[c][:GHOST_ROWS]
            v_send_s[step, c] = got[c][GHOST_ROWS:]

    got = take(pos, own_rows, sids[...])
    for c in range(3):
        p_send_m[c] = got[c][:GHOST_ROWS]
        p_send_s[c] = got[c][GHOST_ROWS:]
    stage_velocity(0)

    pl.semaphore_wait(barrier, peers + 1)
    for copy in position_copies + velocity_copies(0):
        copy.start()

    lax.fori_loop(0, blocks, rows_of_elems, 0)

    def make_onehot(row, carry):
        lane = lax.broadcasted_iota(jnp.int32, (2 * SEG, SEG), 0)
        for i in range(4):
            index = ids[i, pl.ds(row, 1), :]
            low = lax.bitwise_and(index, SEG - 1)
            low = jnp.where(index >= own_rows * SEG, low + SEG, low)
            hot = jnp.where(lane == low, 1.0, 0.0).astype(BF16)
            onehot[:, pl.ds(pl.multiple_of((row * 4 + i) * SEG, SEG), SEG)] = hot
        return carry

    lax.fori_loop(0, blocks, make_onehot, 0)
    for r in range(2 * GHOST_ROWS):
        lane = lax.broadcasted_iota(jnp.int32, (SEG, SEG), 0)
        low = lax.bitwise_and(sids[r : r + 1, :], SEG - 1)
        onehot_back[:, r * SEG : (r + 1) * SEG] = jnp.where(lane == low, 1.0, 0.0).astype(BF16)

    for copy in position_copies:
        copy.wait()
    for c in range(3):
        table[c, :own_rows, :] = pos[c]
        table[c, own_rows : own_rows + GHOST_ROWS, :] = p_recv_m[c]
        table[c, own_rows + GHOST_ROWS :, :] = p_recv_s[c]

    def first_positions(part, carry):
        rows = pl.ds(pl.multiple_of(part * 8, 8), 8)
        for i in range(4):
            got = take(table, own_rows + 2 * GHOST_ROWS, ids[i, rows, :])
            for c in range(3):
                cpos[i, c, rows, :] = got[c]
        return carry

    lax.fori_loop(0, chunks, first_positions, 0)

    high_lane = lax.broadcasted_iota(jnp.int32, (16, SEG), 0)

    def scatter(value_of):
        def one_row(row, carry):
            for i in range(4):
                index = ids[i, pl.ds(row, 1), :]
                high = lax.bitwise_and(lax.shift_right_logical(index, 7), 15)
                here = high_lane == high
                at = pl.ds(pl.multiple_of(i * SEG, SEG), SEG)
                for c in range(3):
                    top, low = halves(jnp.where(here, value_of(i, c, row), 0.0))
                    spread[c * 32 : c * 32 + 16, at] = top
                    spread[c * 32 + 16 : c * 32 + 32, at] = low
            cols = pl.ds(pl.multiple_of(row * 4 * SEG, SEG), 4 * SEG)
            return carry + dot_nt(spread[...], onehot[:, cols])

        total = lax.fori_loop(0, blocks, one_row, jnp.zeros((96, 2 * SEG), F32))
        return [total[c * 32 : c * 32 + 16] + total[c * 32 + 16 : c * 32 + 32] for c in range(3)]

    def one_step(step, step_carry):
        for copy in velocity_copies(step):
            copy.wait()
        for c in range(3):
            vel[c, own_rows : own_rows + GHOST_ROWS, :] = v_recv_m[step, c]
            vel[c, own_rows + GHOST_ROWS :, :] = v_recv_s[step, c]
        advance = jnp.where(step > 0, TIME_STEP, 0.0).astype(F32)

        def shapes(part, carry):
            rows = pl.ds(pl.multiple_of(part * 8, 8), 8)
            a = []
            for i in range(4):
                w = take(vel, own_rows + 2 * GHOST_ROWS, ids[i, rows, :])
                at = []
                for c in range(3):
                    cvel[i, c, rows, :] = w[c]
                    moved = cpos[i, c, rows, :] + advance * w[c]
                    cpos[i, c, rows, :] = moved
                    at.append(moved)
                a.append(at)
            raw = cross(
                [a[2][c] - a[0][c] for c in range(3)], [a[3][c] - a[1][c] for c in range(3)]
            )
            twice = jnp.maximum(jnp.sqrt(dot3(raw, raw)), 1.0)
            area[rows, :] = twice
            for c in range(3):
                n = raw[c] / twice
                centre = 0.25 * (a[0][c] + a[1][c] + a[2][c] + a[3][c])
                nrm[c, rows, :] = n
                geo[rows, c, :] = centre
                geo[rows, 3 + c, :] = n
            return carry

        lax.fori_loop(0, chunks, shapes, 0)

        def block_copy(peer):
            return pltpu.make_async_remote_copy(
                src_ref=send_geo.at[pl.ds(peer * CAP, CAP)],
                dst_ref=recv_geo.at[step, pl.ds(me * CAP, CAP)],
                send_sem=geo_sem.at[0, step],
                recv_sem=geo_sem.at[1, step],
                device_id=(peer, my_sub),
                device_id_type=MESH,
            )

        def send_blocks(hop, carry):
            peer = lax.rem(me + hop, peers)
            for c in range(CAP):
                send_geo[peer * CAP + c] = geo[picks[step, peer * CAP + c]]
            block_copy(peer).start()
            return carry

        lax.fori_loop(1, peers, send_blocks, 0)
        for c in range(CAP):
            recv_geo[step, me * CAP + c] = geo[picks[step, me * CAP + c]]

        def inner_forces(part, carry):
            rows = pl.ds(pl.multiple_of(part * 8, 8), 8)
            a = [[cpos[i, c, rows, :] for c in range(3)] for i in range(4)]
            w = [[cvel[i, c, rows, :] for c in range(3)] for i in range(4)]
            n = [nrm[c, rows, :] for c in range(3)]
            twice = area[rows, :]
            centre = [geo[rows, c, :] for c in range(3)]
            side = [a[1][c] - a[0][c] for c in range(3)]
            length = jnp.maximum(jnp.sqrt(dot3(side, side)), 1.0)
            one = [side[c] / length for c in range(3)]
            two = cross(n, one)
            rel = [[a[i][c] - centre[c] for c in range(3)] for i in range(4)]
            x = [dot3(rel[i], one) for i in range(4)]
            y = [dot3(rel[i], two) for i in range(4)]
            u = [dot3(w[i], one) for i in range(4)]
            v = [dot3(w[i], two) for i in range(4)]
            inverse = 1.0 / twice
            b20, b31 = (y[2] - y[0]) * inverse, (y[1] - y[3]) * inverse
            bx = [b31, b20, -b31, -b20]
            c02, c31 = (x[0] - x[2]) * inverse, (x[3] - x[1]) * inverse
            by = [c31, c02, -c31, -c02]
            exx = b31 * (u[0] - u[2]) + b20 * (u[1] - u[3])
            eyy = c31 * (v[0] - v[2]) + c02 * (v[1] - v[3])
            exy = (
                c31 * (u[0] - u[2]) + c02 * (u[1] - u[3]) + b31 * (v[0] - v[2]) + b20 * (v[1] - v[3])
            )
            s0 = snow[0, rows, :] + TIME_STEP * (PLANE_STIFF * (exx + POISSON * eyy))
            s1 = snow[1, rows, :] + TIME_STEP * (PLANE_STIFF * (POISSON * exx + eyy))
            s2 = snow[2, rows, :] + TIME_STEP * (SHEAR_STIFF * exy)
            snow[0, rows, :] = s0
            snow[1, rows, :] = s1
            snow[2, rows, :] = s2
            half = 0.5 * twice
            hx = x[0] - x[1] + x[2] - x[3]
            hy = y[0] - y[1] + y[2] - y[3]
            signs = (1.0, -1.0, 1.0, -1.0)
            g = [signs[i] - hx * bx[i] - hy * by[i] for i in range(4)]
            r = [
                HOURGLASS * (g[0] * w[0][c] + g[1] * w[1][c] + g[2] * w[2][c] + g[3] * w[3][c])
                for c in range(3)
            ]
            for i in range(4):
                fx = half * (bx[i] * s0 + by[i] * s2)
                fy = half * (by[i] * s1 + bx[i] * s2)
                for c in range(3):
                    fint[i, c, rows, :] = -(fx * one[c] + fy * two[c] + g[i] * r[c])
            return carry

        lax.fori_loop(0, chunks, inner_forces, 0)
        node_force = scatter(lambda i, c, row: fint[i, c, pl.ds(row, 1), :])

        def columns(j, carry):
            for c in range(3):
                row = jnp.broadcast_to(pos[c, pl.ds(j, 1), :], (SEG, SEG))
                pcol[c, j] = jnp.transpose(row)
            for k in range(cands):
                row = pair_mask[step, pl.ds(k, 1), lanes_of(j)].astype(F32) * PENALTY
                mcol[k, j] = jnp.transpose(jnp.broadcast_to(row, (SEG, SEG)))
            return carry

        lax.fori_loop(0, own_rows, columns, 0)

        slot_row = lax.broadcasted_iota(jnp.int32, (slots, pairs * 8), 0)
        slot_row = jnp.where(slot_row < peers, slot_row * CAP, (slot_row - peers) * CAP + 1)
        slot_hot = jnp.where(slot_row == bucket_lanes[pl.ds(step, 1), :], 1.0, 0.0).astype(BF16)

        everything = pl.ds(0, slots - CAP)
        whole = pltpu.make_async_remote_copy(
            src_ref=send_geo.at[everything],
            dst_ref=recv_geo.at[step, everything],
            send_sem=geo_sem.at[0, step],
            recv_sem=geo_sem.at[1, step],
            device_id=mesh_next,
            device_id_type=MESH,
        )
        whole.wait_recv()

        def contact(j, carry):
            normals = []
            for k in range(cands):
                block = recv_geo[step, buckets[step, k * own_rows + j]]
                rows = [jnp.broadcast_to(block[q : q + 1], (16, SEG)) for q in range(6)]
                down = [-rows[3 + c] for c in range(3)]
                normals.append(block[3:6])
                total = jnp.zeros((8, SEG), F32)
                for part in range(SEG // 16):
                    at = slice(part * 16, part * 16 + 16)
                    o = [pcol[c, j, at, :] - rows[c] for c in range(3)]
                    depth = dot3(o, down)
                    reach = depth * depth - dot3(o, o)
                    weight = (
                        jnp.maximum(depth, 0.0) * jnp.exp2(reach * EXP2_SCALE) * mcol[k, j, at, :]
                    )
                    total = total + weight[:8] + weight[8:]
                    top, low = halves(weight)
                    wtop[at, k * SEG : (k + 1) * SEG] = top
                    wlow[at, k * SEG : (k + 1) * SEG] = low
                wsum[pl.ds(pl.multiple_of((k * own_rows + j) * 8, 8), 8), :] = total
            zeros = jnp.zeros((5, cands * SEG), F32)
            flat = jnp.concatenate([jnp.concatenate(normals, axis=1), zeros], axis=0)
            top, low = halves(flat)
            both = jnp.concatenate([top.astype(F32), low.astype(F32)], axis=0).astype(BF16)
            force = dot_nt(both, wtop[...])
            rest = dot_nt(both, wlow[...])
            force = force[:8] + force[8:] + rest[:8]
            for c in range(3):
                slave[c, pl.ds(j, 1), :] = force[c : c + 1]
            return carry

        lax.fori_loop(0, own_rows, contact, 0)

        top, low = halves(wsum[...])
        slot_sum = jnp.dot(slot_hot, top, preferred_element_type=F32) + jnp.dot(
            slot_hot, low, preferred_element_type=F32
        )
        for c in range(CAP):
            ret_send[step, :, c, :] = slot_sum[c * peers : (c + 1) * peers]

        def return_copy(peer):
            return pltpu.make_async_remote_copy(
                src_ref=ret_send.at[step, peer],
                dst_ref=ret_recv.at[step, me],
                send_sem=ret_sem.at[0, step],
                recv_sem=ret_sem.at[1, step],
                device_id=(peer, my_sub),
                device_id_type=MESH,
            )

        def send_back(hop, carry):
            return_copy(lax.rem(me + hop, peers)).start()
            return carry

        lax.fori_loop(1, peers, send_back, 0)
        ret_recv[step, me] = ret_send[step, me]
        pick_hot = lax.broadcasted_iota(jnp.int32, (blocks, slots), 0)
        pick_hot = jnp.where(pick_hot == pick_lanes[pl.ds(step, 1), :], 1.0, 0.0).astype(BF16)
        others = pl.ds(0, peers - 1)
        back = pltpu.make_async_remote_copy(
            src_ref=ret_send.at[step, others],
            dst_ref=ret_recv.at[step, others],
            send_sem=ret_sem.at[0, step],
            recv_sem=ret_sem.at[1, step],
            device_id=mesh_next,
            device_id_type=MESH,
        )
        back.wait_recv()
        returned = jnp.concatenate([ret_recv[step, :, c, :] for c in range(CAP)], axis=0)
        top, low = halves(returned)
        press = jnp.dot(pick_hot, top, preferred_element_type=F32) + jnp.dot(
            pick_hot, low, preferred_element_type=F32
        )
        for c in range(3):
            fint[0, c] = -0.25 * nrm[c] * press
        react = scatter(lambda i, c, row: fint[0, c, pl.ds(row, 1), :])
        force = [node_force[c] + react[c] for c in range(3)]
        for c in range(3):
            f_send_m[step, c] = force[c][:GHOST_ROWS, SEG:]
            f_send_s[step, c] = force[c][GHOST_ROWS : 2 * GHOST_ROWS, SEG:]
        back_copies = force_copies(step)
        for copy in back_copies:
            copy.start()
        for copy in back_copies:
            copy.wait()
        terms = []
        for c in range(3):
            came = jnp.concatenate([f_recv_m[step, c], f_recv_s[step, c]], axis=0)
            tops, lows = [], []
            for r in range(2 * GHOST_ROWS):
                high = lax.shift_right_logical(sids[r : r + 1, :], 7)
                top, low = halves(jnp.where(high_lane == high, came[r : r + 1], 0.0))
                tops.append(top)
                lows.append(low)
            terms.append(jnp.concatenate(tops, axis=1))
            terms.append(jnp.concatenate(lows, axis=1))
        added = dot_nt(jnp.concatenate(terms, axis=0), onehot_back[...])
        for c in range(3):
            own = force[c][:own_rows, :SEG]
            own = own + added[c * 32 : c * 32 + own_rows] + added[c * 32 + 16 : c * 32 + 16 + own_rows]
            now = vel[c, :own_rows, :] + TIME_STEP * (own + slave[c]) / mass[...]
            vel[c, :own_rows, :] = now
            pos[c] = pos[c] + TIME_STEP * now
        whole.wait_send()
        back.wait_send()

        @pl.when(step < STEPS - 1)
        def _():
            stage_velocity(step + 1)
            for copy in velocity_copies(step + 1):
                copy.start()

        return step_carry

    lax.fori_loop(0, STEPS, one_step, 0)
    vel_out[...] = vel[:, :own_rows, :]
    stress_out[...] = snow[...]


def per_device(
    coords, veloc, node_mass, stress, connect, send_mesh, send_sub, send_pick, bucket_list, pair_mask
):
    peers = lax.axis_size("mesh")
    nodes = coords.shape[1]
    elems = stress.shape[1]
    own_rows, blocks = nodes // SEG, elems // SEG
    cands = bucket_list.shape[1]
    slots = send_pick.shape[1]
    pairs = cands * own_rows
    flat_list = bucket_list.reshape(STEPS, pairs)
    bucket_lanes = jnp.repeat(flat_list, 8, axis=1)
    pick_lanes = send_pick.reshape(STEPS, peers, CAP).transpose(0, 2, 1).reshape(STEPS, slots)
    table_rows = own_rows + 2 * GHOST_ROWS
    ghost = (3, GHOST_ROWS, SEG)
    in_vmem = pl.BlockSpec(memory_space=pltpu.VMEM)
    in_smem = pl.BlockSpec(memory_space=pltpu.SMEM)
    v = pltpu.VMEM
    vel_rows, stress_rows = pl.pallas_call(
        functools.partial(kernel, own_rows, blocks, cands),
        out_shape=(
            jax.ShapeDtypeStruct((3, own_rows, SEG), F32),
            jax.ShapeDtypeStruct((3, blocks, SEG), F32),
        ),
        in_specs=[in_vmem] * 7 + [in_smem] * 2 + [in_vmem] * 3,
        out_specs=(in_vmem, in_vmem),
        scratch_shapes=[
            v((4, blocks, SEG), jnp.int32),
            v((2 * GHOST_ROWS, SEG), jnp.int32),
            v((3, own_rows, SEG), F32),
            v((3, table_rows, SEG), F32),
            v((own_rows, SEG), F32),
            v((4, 3, blocks, SEG), F32),
            v((4, 3, blocks, SEG), F32),
            v((3, blocks, SEG), F32),
            v((3, blocks, SEG), F32),
            v((blocks, SEG), F32),
            v((blocks, 6, SEG), F32),
            v((slots, 6, SEG), F32),
            v((STEPS, slots, 6, SEG), F32),
            v((2 * SEG, 4 * elems), BF16),
            v((SEG, 2 * GHOST_ROWS * SEG), BF16),
            v((96, 4 * SEG), BF16),
            v((4, 3, blocks, SEG), F32),
            v((3, table_rows, SEG), F32),
            v((3, own_rows, SEG, SEG), F32),
            v((cands, own_rows, SEG, SEG), F32),
            v((SEG, cands * SEG), BF16),
            v((SEG, cands * SEG), BF16),
            v((pairs * 8, SEG), F32),
            v((3, own_rows, SEG), F32),
            v((STEPS, peers, CAP, SEG), F32),
            v((STEPS, peers, CAP, SEG), F32),
            v(ghost, F32),
            v(ghost, F32),
            v(ghost, F32),
            v(ghost, F32),
            v((STEPS,) + ghost, F32),
            v((STEPS,) + ghost, F32),
            v((STEPS,) + ghost, F32),
            v((STEPS,) + ghost, F32),
            v((STEPS,) + ghost, F32),
            v((STEPS,) + ghost, F32),
            v((STEPS,) + ghost, F32),
            v((STEPS,) + ghost, F32),
            pltpu.SemaphoreType.DMA((4 + STEPS * 8,)),
            pltpu.SemaphoreType.DMA((2, STEPS)),
            pltpu.SemaphoreType.DMA((2, STEPS)),
        ],
        compiler_params=pltpu.CompilerParams(
            collective_id=0, has_side_effects=True, vmem_limit_bytes=56 * 1024 * 1024
        ),
    )(
        coords,
        veloc,
        node_mass.reshape(1, nodes),
        stress,
        connect,
        send_mesh.reshape(1, -1),
        send_sub.reshape(1, -1),
        send_pick,
        flat_list,
        pick_lanes,
        bucket_lanes,
        pair_mask,
    )
    return vel_rows.reshape(3, nodes), stress_rows.reshape(3, elems)


def solution(mesh):
    both = ("mesh", "sub")
    return jax.shard_map(
        per_device,
        mesh=mesh,
        in_specs=(
            P(None, both),
            P(None, both),
            P(both),
            P(None, both),
            P(None, both),
            P(both),
            P(both),
            P(None, both),
            P(None, None, both),
            P(None, None, both),
        ),
        out_specs=(P(None, both), P(None, both)),
        check_vma=False,
    )
```

profile of v0, /device:TPU:1, one launch (start us, length us, event | category | flops | bytes accessed | tf_op | source)
XLA Modules:
  0.0 182.9 jit_solution(768084695664315440)
XLA Ops:
  0.6 0.8 reshape.34.buckets
  1.4 0.0 copy-start.1
  1.4 0.1 broadcast_in_dim.3
  1.5 0.5 copy-done.1
  2.0 0.0 copy-start.2
  2.0 0.7 reshape.37.bucket_lanes
  2.7 0.0 copy-done.2
  2.7 0.1 copy.13
  2.8 0.1 copy.14
  2.9 0.7 reshape.36.pick_lanes
  3.6 177.2 %shard_map.113 = (f32[3,16,128]{2,1,0:T(8,128)}, f32[3,32,128]{2,1,0:T(8,128)}) custom-call(f32[3,2048]{1,0:T(4,128)} %coords.1, f32[3,2048]{1,0:T(4,128)} %veloc.1, f32[1,2048]{1,0:T(1,128)} %bitcast.19, f32[3,4096]{1,0:T(4,128)} %stress_in.1, s32[4,4096]{1,0:T(4,128)} %connect.1, s32[1,512]{1,0:T(1,128)} %bitcast.20, s32[1,512]{1,0:T(1,128)} %bitcast.21, ...), custom_call_target="tpu_custom_call" | custom-call | tf_op jit(solution)/shard_map/pallas_call | solution.py:539
  180.8 0.0 copy-start
  180.8 1.5 copy.19
  182.2 0.0 copy-done
  182.2 0.6 copy.20
Async XLA Ops:
  1.4 0.6 copy-start.1
  2.0 0.7 copy-start.2
  180.8 1.5 copy-start
where the time goes:
time: 183 us
  Pallas kernels  177 us (97%)
  local copies, waits for them, and re-layouts  5.06 us (3%)
    pallas_call x1, Pallas kernels, per_device(): pl.pallas_call(functools.partial(kernel, own_rows, blocks, cands), out_sh...  177 us

commit v1 on v0

--- a/solution.py
+++ b/solution.py
@@ -81,13 +81,19 @@
     recv_geo,
     onehot,
     onehot_back,
+    rowhot,
     spread,
-    fint,
+    ftop,
+    flow,
     table,
     pcol,
     mcol,
-    wtop,
-    wlow,
+    wtop_a,
+    wlow_a,
+    normals_a,
+    wtop_b,
+    wlow_b,
+    normals_b,
     wsum,
     slave,
     ret_send,
@@ -212,15 +218,22 @@
         copy.start()
 
     lax.fori_loop(0, blocks, rows_of_elems, 0)
+    for ref in (wtop_b, wlow_b, normals_b):
+        ref[...] = jnp.zeros(ref.shape, BF16)
+
+    high_lane = lax.broadcasted_iota(jnp.int32, (16, SEG), 0)
+    ghost_lane = lax.bitwise_and(high_lane, 7) + own_rows
 
     def make_onehot(row, carry):
-        lane = lax.broadcasted_iota(jnp.int32, (2 * SEG, SEG), 0)
+        lane = lax.broadcasted_iota(jnp.int32, (SEG, SEG), 0)
         for i in range(4):
             index = ids[i, pl.ds(row, 1), :]
             low = lax.bitwise_and(index, SEG - 1)
-            low = jnp.where(index >= own_rows * SEG, low + SEG, low)
-            hot = jnp.where(lane == low, 1.0, 0.0).astype(BF16)
-            onehot[:, pl.ds(pl.multiple_of((row * 4 + i) * SEG, SEG), SEG)] = hot
+            high = lax.shift_right_logical(index, 7)
+            cols = pl.ds(pl.multiple_of((row * 4 + i) * SEG, SEG), SEG)
+            onehot[:, cols] = jnp.where(lane == low, 1.0, 0.0).astype(BF16)
+            rowhot[:16, cols] = jnp.where(high_lane == high, 1.0, 0.0).astype(BF16)
+            rowhot[16:, cols] = jnp.where(ghost_lane == high, 1.0, 0.0).astype(BF16)
         return carry
 
     lax.fori_loop(0, blocks, make_onehot, 0)
@@ -246,24 +259,51 @@
 
     lax.fori_loop(0, chunks, first_positions, 0)
 
-    high_lane = lax.broadcasted_iota(jnp.int32, (16, SEG), 0)
-
-    def scatter(value_of):
-        def one_row(row, carry):
-            for i in range(4):
-                index = ids[i, pl.ds(row, 1), :]
-                high = lax.bitwise_and(lax.shift_right_logical(index, 7), 15)
-                here = high_lane == high
-                at = pl.ds(pl.multiple_of(i * SEG, SEG), SEG)
-                for c in range(3):
-                    top, low = halves(jnp.where(here, value_of(i, c, row), 0.0))
-                    spread[c * 32 : c * 32 + 16, at] = top
-                    spread[c * 32 + 16 : c * 32 + 32, at] = low
-            cols = pl.ds(pl.multiple_of(row * 4 * SEG, SEG), 4 * SEG)
+    def scatter(corners):
+        def one_part(part, carry):
+            def one_row(r, inner):
+                row = part * 8 + r
+                values = []
+                for i in range(corners):
+                    for c in range(3):
+                        top = ftop[i, c, pl.ds(row, 1), :]
+                        low = flow[i, c, pl.ds(row, 1), :]
+                        top8 = jnp.broadcast_to(top, (8, SEG))
+                        low8 = jnp.broadcast_to(low, (8, SEG))
+                        values.append(
+                            (
+                                jnp.concatenate([top8, top8], axis=0).astype(BF16),
+                                jnp.concatenate([low8, low8], axis=0).astype(BF16),
+                                jnp.concatenate([top8, low8], axis=0).astype(BF16),
+                            )
+                        )
+                for i in range(4):
+                    cols = pl.ds(pl.multiple_of((row * 4 + i) * SEG, SEG), SEG)
+                    at = pl.ds(pl.multiple_of((r * 4 + i) * SEG, SEG), SEG)
+                    here = rowhot[:16, cols]
+                    away = rowhot[16:, cols]
+                    for c in range(3):
+                        top, low, both = values[(i if corners > 1 else 0) * 3 + c]
+                        spread[c * 32 : c * 32 + 16, at] = here * top
+                        spread[c * 32 + 16 : c * 32 + 32, at] = here * low
+                        spread[96 + c * 16 : 112 + c * 16, at] = away * both
+                return inner
+
+            lax.fori_loop(0, 8, one_row, 0)
+            cols = pl.ds(pl.multiple_of(part * 32 * SEG, 32 * SEG), 32 * SEG)
             return carry + dot_nt(spread[...], onehot[:, cols])
 
-        total = lax.fori_loop(0, blocks, one_row, jnp.zeros((96, 2 * SEG), F32))
-        return [total[c * 32 : c * 32 + 16] + total[c * 32 + 16 : c * 32 + 32] for c in range(3)]
+        total = lax.fori_loop(0, chunks, one_part, jnp.zeros((144, SEG), F32))
+        own = [total[c * 32 : c * 32 + 16] + total[c * 32 + 16 : c * 32 + 32] for c in range(3)]
+        ghost = [
+            total[96 + c * 16 : 104 + c * 16] + total[104 + c * 16 : 112 + c * 16] for c in range(3)
+        ]
+        return own + ghost
+
+    def store_halves(i, c, rows, value):
+        top = value.astype(BF16).astype(F32)
+        ftop[i, c, rows, :] = top
+        flow[i, c, rows, :] = value - top
 
     def one_step(step, step_carry):
         for copy in velocity_copies(step):
@@ -366,11 +406,11 @@
                 fx = half * (bx[i] * s0 + by[i] * s2)
                 fy = half * (by[i] * s1 + bx[i] * s2)
                 for c in range(3):
-                    fint[i, c, rows, :] = -(fx * one[c] + fy * two[c] + g[i] * r[c])
+                    store_halves(i, c, rows, -(fx * one[c] + fy * two[c] + g[i] * r[c]))
             return carry
 
         lax.fori_loop(0, chunks, inner_forces, 0)
-        node_force = scatter(lambda i, c, row: fint[i, c, pl.ds(row, 1), :])
+        node_force = scatter(4)
 
         def columns(j, carry):
             for c in range(3):
@@ -398,7 +438,7 @@
         )
         whole.wait_recv()
 
-        def contact(j, carry):
+        def contact(j, wtop, wlow, normals_at):
             normals = []
             for k in range(cands):
                 block = recv_geo[step, buckets[step, k * own_rows + j]]
@@ -421,16 +461,29 @@
                 wsum[pl.ds(pl.multiple_of((k * own_rows + j) * 8, 8), 8), :] = total
             zeros = jnp.zeros((5, cands * SEG), F32)
             flat = jnp.concatenate([jnp.concatenate(normals, axis=1), zeros], axis=0)
-            top, low = halves(flat)
-            both = jnp.concatenate([top.astype(F32), low.astype(F32)], axis=0).astype(BF16)
+            top = flat.astype(BF16).astype(F32)
+            normals_at[...] = jnp.concatenate([top, flat - top], axis=0).astype(BF16)
+
+        def push(j, wtop, wlow, normals_at):
+            both = normals_at[...]
             force = dot_nt(both, wtop[...])
             rest = dot_nt(both, wlow[...])
             force = force[:8] + force[8:] + rest[:8]
             for c in range(3):
                 slave[c, pl.ds(j, 1), :] = force[c : c + 1]
+
+        even = (wtop_a, wlow_a, normals_a)
+        odd = (wtop_b, wlow_b, normals_b)
+
+        def contact_pair(half, carry):
+            push(jnp.maximum(2 * half - 1, 0), *odd)
+            contact(2 * half, *even)
+            push(2 * half, *even)
+            contact(2 * half + 1, *odd)
             return carry
 
-        lax.fori_loop(0, own_rows, contact, 0)
+        lax.fori_loop(0, own_rows // 2, contact_pair, 0)
+        push(own_rows - 1, *odd)
 
         top, low = halves(wsum[...])
         slot_sum = jnp.dot(slot_hot, top, preferred_element_type=F32) + jnp.dot(
@@ -473,12 +526,12 @@
             pick_hot, low, preferred_element_type=F32
         )
         for c in range(3):
-            fint[0, c] = -0.25 * nrm[c] * press
-        react = scatter(lambda i, c, row: fint[0, c, pl.ds(row, 1), :])
-        force = [node_force[c] + react[c] for c in range(3)]
-        for c in range(3):
-            f_send_m[step, c] = force[c][:GHOST_ROWS, SEG:]
-            f_send_s[step, c] = force[c][GHOST_ROWS : 2 * GHOST_ROWS, SEG:]
+            store_halves(0, c, slice(None), -0.25 * nrm[c] * press)
+        react = scatter(1)
+        force = [node_force[c] + react[c] for c in range(6)]
+        for c in range(3):
+            f_send_m[step, c] = force[3 + c][:GHOST_ROWS]
+            f_send_s[step, c] = force[3 + c][GHOST_ROWS:]
         back_copies = force_copies(step)
         for copy in back_copies:
             copy.start()
@@ -497,7 +550,7 @@
             terms.append(jnp.concatenate(lows, axis=1))
         added = dot_nt(jnp.concatenate(terms, axis=0), onehot_back[...])
         for c in range(3):
-            own = force[c][:own_rows, :SEG]
+            own = force[c]
             own = own + added[c * 32 : c * 32 + own_rows] + added[c * 32 + 16 : c * 32 + 16 + own_rows]
             now = vel[c, :own_rows, :] + TIME_STEP * (own + slave[c]) / mass[...]
             vel[c, :own_rows, :] = now
@@ -558,15 +611,21 @@
             v((blocks, 6, SEG), F32),
             v((slots, 6, SEG), F32),
             v((STEPS, slots, 6, SEG), F32),
-            v((2 * SEG, 4 * elems), BF16),
+            v((SEG, 4 * elems), BF16),
             v((SEG, 2 * GHOST_ROWS * SEG), BF16),
-            v((96, 4 * SEG), BF16),
+            v((32, 4 * elems), BF16),
+            v((144, 32 * SEG), BF16),
+            v((4, 3, blocks, SEG), F32),
             v((4, 3, blocks, SEG), F32),
             v((3, table_rows, SEG), F32),
             v((3, own_rows, SEG, SEG), F32),
             v((cands, own_rows, SEG, SEG), F32),
             v((SEG, cands * SEG), BF16),
             v((SEG, cands * SEG), BF16),
+            v((16, cands * SEG), BF16),
+            v((SEG, cands * SEG), BF16),
+            v((SEG, cands * SEG), BF16),
+            v((16, cands * SEG), BF16),
             v((pairs * 8, SEG), F32),
             v((3, own_rows, SEG), F32),
             v((STEPS, peers, CAP, SEG), F32),

time: 183 us -> 160 us (0.87)
  Pallas kernels: 177 us -> 154 us
    pallas_call x1, Pallas kernels: 177 us -> 154 us  [per_device(): pl.pallas_call(functools.partial(kernel, own_rows, blocks, cands), out_sh...]
where the time goes in v1:
time: 160 us; the launch traced here: 159 us
  Pallas kernels  154 us (96%)
  local copies, waits for them, and re-layouts  5.06 us (3%)
    pallas_call x1, Pallas kernels, per_device(): pl.pallas_call(functools.partial(kernel, own_rows, blocks, cands), out_sh...  154 us

profile of v1, /device:TPU:1, one launch (start us, length us, event | category | flops | bytes accessed | tf_op | source)
XLA Modules:
  0.0 159.3 jit_solution(9645265302167348131)
XLA Ops:
  0.6 0.8 reshape.34.buckets
  1.4 0.0 copy-start.1
  1.4 0.1 broadcast_in_dim.3
  1.5 0.5 copy-done.1
  2.0 0.0 copy-start.2
  2.0 0.7 reshape.37.bucket_lanes
  2.7 0.0 copy-done.2
  2.7 0.1 copy.13
  2.8 0.1 copy.14
  2.9 0.7 reshape.36.pick_lanes
  3.6 153.6 %shard_map.113 = (f32[3,16,128]{2,1,0:T(8,128)}, f32[3,32,128]{2,1,0:T(8,128)}) custom-call(f32[3,2048]{1,0:T(4,128)} %coords.1, f32[3,2048]{1,0:T(4,128)} %veloc.1, f32[1,2048]{1,0:T(1,128)} %bitcast.19, f32[3,4096]{1,0:T(4,128)} %stress_in.1, s32[4,4096]{1,0:T(4,128)} %connect.1, s32[1,512]{1,0:T(1,128)} %bitcast.20, s32[1,512]{1,0:T(1,128)} %bitcast.21, ...), custom_call_target="tpu_custom_call" | custom-call | tf_op jit(solution)/shard_map/pallas_call | solution.py:592
  157.2 0.0 copy-start
  157.2 1.5 copy.19
  158.7 0.0 copy-done
  158.7 0.6 copy.20
Async XLA Ops:
  1.4 0.6 copy-start.1
  2.0 0.7 copy-start.2
  157.2 1.5 copy-start

commit v2 on v1

--- a/solution.py
+++ b/solution.py
@@ -61,8 +61,7 @@
     send_sub,
     picks,
     buckets,
-    pick_lanes,
-    bucket_lanes,
+    pick_rows,
     pair_mask,
     vel_out,
     stress_out,
@@ -95,6 +94,7 @@
     wlow_b,
     normals_b,
     wsum,
+    named,
     slave,
     ret_send,
     ret_recv,
@@ -126,6 +126,27 @@
     chunks = blocks // 8
     pairs = cands * own_rows
 
+    ring_x, ring_z = 4, peers // 8
+    my_core, my_z, my_x = me % 2, me // 2 % ring_z, me // (2 * ring_z)
+
+    def spread_out(ring, turn):
+        return ring // 2 + (turn + 1) // 2 * (1 - 2 * (turn % 2))
+
+    def each_partner(act):
+        def one_z(turn, carry):
+            z = lax.rem(my_z + spread_out(ring_z, turn), ring_z)
+            for turn_x in range(ring_x):
+                x = lax.rem(my_x + spread_out(ring_x, turn_x), ring_x)
+                chip = (x * ring_z + z) * 2
+                act(chip + 1 - my_core)
+                if turn_x < ring_x - 1:
+                    act(chip + my_core)
+                else:
+                    pl.when(turn < ring_z - 1)(lambda chip=chip: act(chip + my_core))
+            return carry
+
+        lax.fori_loop(0, ring_z, one_z, 0)
+
     barrier = pltpu.get_barrier_semaphore()
 
     def greet(hop, carry):
@@ -350,14 +371,12 @@
                 device_id_type=MESH,
             )
 
-        def send_blocks(hop, carry):
-            peer = lax.rem(me + hop, peers)
+        def send_blocks(peer):
             for c in range(CAP):
                 send_geo[peer * CAP + c] = geo[picks[step, peer * CAP + c]]
             block_copy(peer).start()
-            return carry
-
-        lax.fori_loop(1, peers, send_blocks, 0)
+
+        each_partner(send_blocks)
         for c in range(CAP):
             recv_geo[step, me * CAP + c] = geo[picks[step, me * CAP + c]]
 
@@ -423,9 +442,17 @@
 
         lax.fori_loop(0, own_rows, columns, 0)
 
-        slot_row = lax.broadcasted_iota(jnp.int32, (slots, pairs * 8), 0)
-        slot_row = jnp.where(slot_row < peers, slot_row * CAP, (slot_row - peers) * CAP + 1)
-        slot_hot = jnp.where(slot_row == bucket_lanes[pl.ds(step, 1), :], 1.0, 0.0).astype(BF16)
+        slot_lane = lax.broadcasted_iota(jnp.int32, (8, slots), 1)
+        slot_lane = jnp.where(slot_lane < peers, slot_lane * CAP, (slot_lane - peers) * CAP + 1)
+
+        def name_slots(j, carry):
+            for k in range(cands):
+                rows = pl.ds(pl.multiple_of((k * own_rows + j) * 8, 8), 8)
+                named[rows, :] = jnp.where(slot_lane == buckets[step, k, j], 1.0, 0.0)
+            return carry
+
+        lax.fori_loop(0, own_rows, name_slots, 0)
+        slot_hot = jnp.transpose(named[...]).astype(BF16)
 
         everything = pl.ds(0, slots - CAP)
         whole = pltpu.make_async_remote_copy(
@@ -441,7 +468,7 @@
         def contact(j, wtop, wlow, normals_at):
             normals = []
             for k in range(cands):
-                block = recv_geo[step, buckets[step, k * own_rows + j]]
+                block = recv_geo[step, buckets[step, k, j]]
                 rows = [jnp.broadcast_to(block[q : q + 1], (16, SEG)) for q in range(6)]
                 down = [-rows[3 + c] for c in range(3)]
                 normals.append(block[3:6])
@@ -502,14 +529,14 @@
                 device_id_type=MESH,
             )
 
-        def send_back(hop, carry):
-            return_copy(lax.rem(me + hop, peers)).start()
-            return carry
-
-        lax.fori_loop(1, peers, send_back, 0)
+        each_partner(lambda peer: return_copy(peer).start())
         ret_recv[step, me] = ret_send[step, me]
         pick_hot = lax.broadcasted_iota(jnp.int32, (blocks, slots), 0)
-        pick_hot = jnp.where(pick_hot == pick_lanes[pl.ds(step, 1), :], 1.0, 0.0).astype(BF16)
+        order = lax.broadcasted_iota(jnp.int32, (8, slots), 1)
+        order = jnp.where(order < peers, order * CAP, (order - peers) * CAP + 1)
+        picked = jnp.broadcast_to(pick_rows[pl.ds(step, 1), :], (8, slots))
+        picked = jnp.take_along_axis(picked, order, axis=1, mode="promise_in_bounds")
+        pick_hot = jnp.where(pick_hot == picked[:1], 1.0, 0.0).astype(BF16)
         others = pl.ds(0, peers - 1)
         back = pltpu.make_async_remote_copy(
             src_ref=ret_send.at[step, others],
@@ -567,8 +594,19 @@
         return step_carry
 
     lax.fori_loop(0, STEPS, one_step, 0)
-    vel_out[...] = vel[:, :own_rows, :]
-    stress_out[...] = snow[...]
+
+    def velocity_lanes(row, carry):
+        for c in range(3):
+            vel_out[pl.ds(c, 1), lanes_of(row)] = vel[c, pl.ds(row, 1), :]
+        return carry
+
+    def stress_lanes(row, carry):
+        for c in range(3):
+            stress_out[pl.ds(c, 1), lanes_of(row)] = snow[c, pl.ds(row, 1), :]
+        return carry
+
+    lax.fori_loop(0, own_rows, velocity_lanes, 0)
+    lax.fori_loop(0, blocks, stress_lanes, 0)
 
 
 def per_device(
@@ -581,21 +619,18 @@
     cands = bucket_list.shape[1]
     slots = send_pick.shape[1]
     pairs = cands * own_rows
-    flat_list = bucket_list.reshape(STEPS, pairs)
-    bucket_lanes = jnp.repeat(flat_list, 8, axis=1)
-    pick_lanes = send_pick.reshape(STEPS, peers, CAP).transpose(0, 2, 1).reshape(STEPS, slots)
     table_rows = own_rows + 2 * GHOST_ROWS
     ghost = (3, GHOST_ROWS, SEG)
     in_vmem = pl.BlockSpec(memory_space=pltpu.VMEM)
     in_smem = pl.BlockSpec(memory_space=pltpu.SMEM)
     v = pltpu.VMEM
-    vel_rows, stress_rows = pl.pallas_call(
+    return pl.pallas_call(
         functools.partial(kernel, own_rows, blocks, cands),
         out_shape=(
-            jax.ShapeDtypeStruct((3, own_rows, SEG), F32),
-            jax.ShapeDtypeStruct((3, blocks, SEG), F32),
+            jax.ShapeDtypeStruct((3, nodes), F32),
+            jax.ShapeDtypeStruct((3, elems), F32),
         ),
-        in_specs=[in_vmem] * 7 + [in_smem] * 2 + [in_vmem] * 3,
+        in_specs=[in_vmem] * 7 + [in_smem] * 2 + [in_vmem] * 2,
         out_specs=(in_vmem, in_vmem),
         scratch_shapes=[
             v((4, blocks, SEG), jnp.int32),
@@ -627,6 +662,7 @@
             v((SEG, cands * SEG), BF16),
             v((16, cands * SEG), BF16),
             v((pairs * 8, SEG), F32),
+            v((pairs * 8, slots), F32),
             v((3, own_rows, SEG), F32),
             v((STEPS, peers, CAP, SEG), F32),
             v((STEPS, peers, CAP, SEG), F32),
@@ -658,12 +694,10 @@
         send_mesh.reshape(1, -1),
         send_sub.reshape(1, -1),
         send_pick,
-        flat_list,
-        pick_lanes,
-        bucket_lanes,
+        bucket_list,
+        send_pick,
         pair_mask,
     )
-    return vel_rows.reshape(3, nodes), stress_rows.reshape(3, elems)
 
 
 def solution(mesh):

time: 160 us -> 152 us (0.950)
  Pallas kernels: 154 us -> 149 us
  local copies, waits for them, and re-layouts: 5.06 us -> 2.04 us
    pallas_call x1, Pallas kernels: 154 us -> 149 us  [per_device(): pl.pallas_call(functools.partial(kernel, own_rows, blocks, cands), out_sh...]
    reshape x3 -> x0, local copies, waits for them, and re-layouts: 2.18 us -> none  [the longest x1 0.78 us: per_device(): flat_list = bucket_list.reshape(STEPS, pairs)]
where the time goes in v2:
time: 152 us
  Pallas kernels  149 us (98%)
  local copies, waits for them, and re-layouts  2.04 us (1%)
    pallas_call x1, Pallas kernels, per_device(): pl.pallas_call(functools.partial(kernel, own_rows, blocks, cands), out_sh...  149 us

profile of v2, /device:TPU:1, one launch (start us, length us, event | category | flops | bytes accessed | tf_op | source)
XLA Modules:
  0.0 151.8 jit_solution(5673446396511143498)
XLA Ops:
  0.6 149.1 %shard_map.113 = (f32[3,2048]{1,0:T(4,128)}, f32[3,4096]{1,0:T(4,128)}) custom-call(f32[3,2048]{1,0:T(4,128)} %coords.1, f32[3,2048]{1,0:T(4,128)} %veloc.1, f32[1,2048]{1,0:T(1,128)} %bitcast.3, f32[3,4096]{1,0:T(4,128)} %stress_in.1, s32[4,4096]{1,0:T(4,128)} %connect.1, s32[1,512]{1,0:T(1,128)} %bitcast.4, s32[1,512]{1,0:T(1,128)} %bitcast.5, ...), custom_call_target="tpu_custom_call" | custom-call | tf_op jit(solution)/shard_map/pallas_call | solution.py:627
  149.7 0.0 copy-start
  149.8 1.4 copy.14
  151.2 0.0 copy-done
  151.2 0.6 copy.15
Async XLA Ops:
  149.7 1.4 copy-start

commit v3 on v2

--- a/solution.py
+++ b/solution.py
@@ -20,6 +20,7 @@
 PLANE_STIFF = YOUNG / (1.0 - POISSON * POISSON)
 SHEAR_STIFF = YOUNG / (2.0 * (1.0 + POISSON))
 EXP2_SCALE = math.log2(math.e) / REACH
+ROOT_SCALE = math.sqrt(EXP2_SCALE)
 MESH = pl.DeviceIdType.MESH
 F32 = jnp.float32
 BF16 = jnp.bfloat16
@@ -34,6 +35,13 @@
 def halves(value):
     top = value.astype(BF16)
     return top, (value - top.astype(F32)).astype(BF16)
+
+
+def thirds(value):
+    top = value.astype(BF16).astype(F32)
+    rest = value - top
+    mid = rest.astype(BF16).astype(F32)
+    return top, mid, rest - mid
 
 
 def cross(u, v):
@@ -81,12 +89,15 @@
     onehot,
     onehot_back,
     rowhot,
-    spread,
+    spread_a,
+    spread_b,
     ftop,
     flow,
     table,
     pcol,
     mcol,
+    pairs_a,
+    pairs_b,
     wtop_a,
     wlow_a,
     normals_a,
@@ -98,18 +109,27 @@
     slave,
     ret_send,
     ret_recv,
-    p_send_m,
-    p_send_s,
-    p_recv_m,
-    p_recv_s,
-    v_send_m,
-    v_send_s,
-    v_recv_m,
-    v_recv_s,
+    first_send_m,
+    first_send_s,
+    first_recv_m,
+    first_recv_s,
+    sids_m,
+    sids_s,
+    same_m,
+    same_s,
+    values_m,
+    values_s,
+    part,
+    o_send_m,
+    o_send_s,
+    o_recv_m,
+    o_recv_s,
     f_send_m,
     f_send_s,
     f_recv_m,
     f_recv_s,
+    x_recv_m,
+    x_recv_s,
     halo_sem,
     geo_sem,
     ret_sem,
@@ -122,6 +142,8 @@
     mesh_prev = (lax.rem(me + peers - 1, peers), my_sub)
     sub_next = (me, lax.rem(my_sub + 1, subs))
     sub_prev = (me, lax.rem(my_sub + subs - 1, subs))
+    corner_a = (mesh_prev[0], sub_next[1])
+    corner_b = (mesh_next[0], sub_prev[1])
     slots = peers * CAP
     chunks = blocks // 8
     pairs = cands * own_rows
@@ -156,7 +178,7 @@
         return carry
 
     lax.fori_loop(1, peers, greet, 0)
-    for other in (sub_next, sub_prev):
+    for other in (sub_next, sub_prev, corner_a, corner_b):
         pl.semaphore_signal(barrier, inc=1, device_id=other, device_id_type=MESH)
 
     def lanes_of(row):
@@ -166,7 +188,7 @@
         for c in range(3):
             pos[c, pl.ds(row, 1), :] = coords[pl.ds(c, 1), lanes_of(row)]
             vel[c, pl.ds(row, 1), :] = veloc[pl.ds(c, 1), lanes_of(row)]
-        mass[pl.ds(row, 1), :] = mass_in[:, lanes_of(row)]
+        mass[0, pl.ds(row, 1), :] = mass_in[:, lanes_of(row)]
         return carry
 
     def rows_of_elems(row, carry):
@@ -181,13 +203,13 @@
         sids[r : r + 1, :] = send_mesh[:, r * SEG : (r + 1) * SEG]
         sids[GHOST_ROWS + r : GHOST_ROWS + r + 1, :] = send_sub[:, r * SEG : (r + 1) * SEG]
 
-    def take(tables, rows, index):
+    def take(tables, rows, index, comps=3):
         low = lax.bitwise_and(index, SEG - 1)
         high = lax.shift_right_logical(index, 7)
-        found = [jnp.zeros(index.shape, F32) for _ in range(3)]
+        found = [jnp.zeros(index.shape, F32) for _ in range(comps)]
         for r in range(rows):
             here = high == r
-            for c in range(3):
+            for c in range(comps):
                 source = jnp.broadcast_to(tables[c, r : r + 1, :], index.shape)
                 got = jnp.take_along_axis(source, low, axis=1, mode="promise_in_bounds")
                 found[c] = jnp.where(here, got, found[c])
@@ -203,44 +225,38 @@
             device_id_type=MESH,
         )
 
-    def velocity_copies(step):
-        base = 4 + step * 8
+    first_copies = (
+        halo_copy(first_send_m, first_recv_m, 0, mesh_next),
+        halo_copy(first_send_s, first_recv_s, 2, sub_next),
+        halo_copy(sids, sids_m, 4, mesh_next),
+        halo_copy(sids, sids_s, 6, sub_next),
+    )
+
+    def step_copies(step):
+        base = 8 + step * 12
         return (
-            halo_copy(v_send_m.at[step], v_recv_m.at[step], base, mesh_next),
-            halo_copy(v_send_s.at[step], v_recv_s.at[step], base + 2, sub_next),
+            halo_copy(f_send_m.at[step], x_recv_m.at[step], base, corner_a),
+            halo_copy(f_send_s.at[step], x_recv_s.at[step], base + 2, corner_b),
+            halo_copy(f_send_m.at[step], f_recv_m.at[step], base + 4, mesh_prev),
+            halo_copy(f_send_s.at[step], f_recv_s.at[step], base + 6, sub_prev),
+            halo_copy(o_send_m.at[step], o_recv_m.at[step], base + 8, mesh_next),
+            halo_copy(o_send_s.at[step], o_recv_s.at[step], base + 10, sub_next),
         )
 
-    def force_copies(step):
-        base = 4 + step * 8 + 4
-        return (
-            halo_copy(f_send_m.at[step], f_recv_m.at[step], base, mesh_prev),
-            halo_copy(f_send_s.at[step], f_recv_s.at[step], base + 2, sub_prev),
-        )
-
-    position_copies = (
-        halo_copy(p_send_m, p_recv_m, 0, mesh_next),
-        halo_copy(p_send_s, p_recv_s, 2, sub_next),
-    )
-
-    def stage_velocity(step):
-        got = take(vel, own_rows, sids[...])
-        for c in range(3):
-            v_send_m[step, c] = got[c][:GHOST_ROWS]
-            v_send_s[step, c] = got[c][GHOST_ROWS:]
-
-    got = take(pos, own_rows, sids[...])
-    for c in range(3):
-        p_send_m[c] = got[c][:GHOST_ROWS]
-        p_send_s[c] = got[c][GHOST_ROWS:]
-    stage_velocity(0)
-
-    pl.semaphore_wait(barrier, peers + 1)
-    for copy in position_copies + velocity_copies(0):
-        copy.start()
+    firsts = take(pos, own_rows, sids[...]) + take(vel, own_rows, sids[...])
+    for q, got in enumerate(firsts + take(mass, own_rows, sids[...], 1)):
+        first_send_m[q] = got[:GHOST_ROWS]
+        first_send_s[q] = got[GHOST_ROWS:]
 
     lax.fori_loop(0, blocks, rows_of_elems, 0)
     for ref in (wtop_b, wlow_b, normals_b):
         ref[...] = jnp.zeros(ref.shape, BF16)
+    for ref in (values_m, values_s):
+        ref[...] = jnp.zeros(ref.shape, F32)
+
+    pl.semaphore_wait(barrier, peers + 3)
+    for copy in first_copies:
+        copy.start()
 
     high_lane = lax.broadcasted_iota(jnp.int32, (16, SEG), 0)
     ghost_lane = lax.bitwise_and(high_lane, 7) + own_rows
@@ -263,12 +279,26 @@
         low = lax.bitwise_and(sids[r : r + 1, :], SEG - 1)
         onehot_back[:, r * SEG : (r + 1) * SEG] = jnp.where(lane == low, 1.0, 0.0).astype(BF16)
 
-    for copy in position_copies:
+    for copy in first_copies:
         copy.wait()
     for c in range(3):
         table[c, :own_rows, :] = pos[c]
-        table[c, own_rows : own_rows + GHOST_ROWS, :] = p_recv_m[c]
-        table[c, own_rows + GHOST_ROWS :, :] = p_recv_s[c]
+        for got, at in ((first_recv_m, own_rows), (first_recv_s, own_rows + GHOST_ROWS)):
+            table[c, at : at + GHOST_ROWS, :] = got[c]
+            vel[c, at : at + GHOST_ROWS, :] = got[3 + c]
+    ghost_mass = jnp.concatenate([first_recv_m[6], first_recv_s[6]], axis=0)
+
+    def match(hot, lists, first):
+        names = lists[...].astype(F32)
+        for q in range(GHOST_ROWS):
+            mine = names[first + q : first + q + 1]
+            mine = jnp.transpose(jnp.broadcast_to(mine, (SEG, SEG)))
+            for r in range(2 * GHOST_ROWS):
+                same = jnp.where(mine == names[r : r + 1], 1.0, 0.0)
+                hot[q * SEG : (q + 1) * SEG, r * SEG : (r + 1) * SEG] = same.astype(BF16)
+
+    match(same_m, sids_m, 0)
+    match(same_s, sids_s, GHOST_ROWS)
 
     def first_positions(part, carry):
         rows = pl.ds(pl.multiple_of(part * 8, 8), 8)
@@ -281,8 +311,8 @@
     lax.fori_loop(0, chunks, first_positions, 0)
 
     def scatter(corners):
-        def one_part(part, carry):
-            def one_row(r, inner):
+        def build(part, spread):
+            for r in range(8):
                 row = part * 8 + r
                 values = []
                 for i in range(corners):
@@ -300,7 +330,7 @@
                         )
                 for i in range(4):
                     cols = pl.ds(pl.multiple_of((row * 4 + i) * SEG, SEG), SEG)
-                    at = pl.ds(pl.multiple_of((r * 4 + i) * SEG, SEG), SEG)
+                    at = slice((r * 4 + i) * SEG, (r * 4 + i + 1) * SEG)
                     here = rowhot[:16, cols]
                     away = rowhot[16:, cols]
                     for c in range(3):
@@ -308,13 +338,19 @@
                         spread[c * 32 : c * 32 + 16, at] = here * top
                         spread[c * 32 + 16 : c * 32 + 32, at] = here * low
                         spread[96 + c * 16 : 112 + c * 16, at] = away * both
-                return inner
-
-            lax.fori_loop(0, 8, one_row, 0)
+
+        def product(part, spread):
             cols = pl.ds(pl.multiple_of(part * 32 * SEG, 32 * SEG), 32 * SEG)
-            return carry + dot_nt(spread[...], onehot[:, cols])
-
-        total = lax.fori_loop(0, chunks, one_part, jnp.zeros((144, SEG), F32))
+            return dot_nt(spread[...], onehot[:, cols])
+
+        def two_parts(half, carry):
+            build(2 * half + 1, spread_b)
+            carry = carry + product(2 * half, spread_a)
+            build(jnp.minimum(2 * half + 2, chunks - 1), spread_a)
+            return carry + product(2 * half + 1, spread_b)
+
+        build(0, spread_a)
+        total = lax.fori_loop(0, chunks // 2, two_parts, jnp.zeros((144, SEG), F32))
         own = [total[c * 32 : c * 32 + 16] + total[c * 32 + 16 : c * 32 + 32] for c in range(3)]
         ghost = [
             total[96 + c * 16 : 104 + c * 16] + total[104 + c * 16 : 112 + c * 16] for c in range(3)
@@ -327,11 +363,6 @@
         flow[i, c, rows, :] = value - top
 
     def one_step(step, step_carry):
-        for copy in velocity_copies(step):
-            copy.wait()
-        for c in range(3):
-            vel[c, own_rows : own_rows + GHOST_ROWS, :] = v_recv_m[step, c]
-            vel[c, own_rows + GHOST_ROWS :, :] = v_recv_s[step, c]
         advance = jnp.where(step > 0, TIME_STEP, 0.0).astype(F32)
 
         def shapes(part, carry):
@@ -432,11 +463,15 @@
         node_force = scatter(4)
 
         def columns(j, carry):
-            for c in range(3):
-                row = jnp.broadcast_to(pos[c, pl.ds(j, 1), :], (SEG, SEG))
-                pcol[c, j] = jnp.transpose(row)
+            p = [pos[c, pl.ds(j, 1), :] for c in range(3)]
+            one = jnp.ones((1, SEG), F32)
+            top, mid, low = thirds(
+                jnp.concatenate(p + [dot3(p, p), one, jnp.zeros((3, SEG), F32)], axis=0)
+            )
+            pieces = jnp.concatenate([top, top, mid, mid, top, low], axis=0)
+            pcol[j] = jnp.transpose(pieces).astype(BF16)
             for k in range(cands):
-                row = pair_mask[step, pl.ds(k, 1), lanes_of(j)].astype(F32) * PENALTY
+                row = pair_mask[step, pl.ds(k, 1), lanes_of(j)].astype(F32) * (PENALTY / ROOT_SCALE)
                 mcol[k, j] = jnp.transpose(jnp.broadcast_to(row, (SEG, SEG)))
             return carry
 
@@ -465,21 +500,32 @@
         )
         whole.wait_recv()
 
-        def contact(j, wtop, wlow, normals_at):
+        def quadratics(j, both):
+            for k in range(cands):
+                block = recv_geo[step, buckets[step, k, j]]
+                centre, normal = block[:3], block[3:6]
+                along = jnp.sum(centre * normal, axis=0, keepdims=True)
+                square = jnp.sum(centre * centre, axis=0, keepdims=True)
+                nothing = jnp.zeros((1, SEG), F32)
+                blank = jnp.zeros((3, SEG), F32)
+                depth = jnp.concatenate([-normal, nothing, along, blank], axis=0) * ROOT_SCALE
+                far = jnp.concatenate([-2.0 * centre, nothing + 1.0, square, blank], axis=0)
+                top, mid, low = thirds(jnp.concatenate([depth, far * EXP2_SCALE], axis=1))
+                pieces = jnp.concatenate([top, mid, top, mid, low, top], axis=0).astype(BF16)
+                at = slice(k * 2 * SEG, (k + 1) * 2 * SEG)
+                both[:, at] = jnp.dot(pcol[j], pieces, preferred_element_type=F32)
+
+        def contact(j, both, wtop, wlow, normals_at):
             normals = []
             for k in range(cands):
-                block = recv_geo[step, buckets[step, k, j]]
-                rows = [jnp.broadcast_to(block[q : q + 1], (16, SEG)) for q in range(6)]
-                down = [-rows[3 + c] for c in range(3)]
-                normals.append(block[3:6])
+                normals.append(recv_geo[step, buckets[step, k, j]][3:6])
                 total = jnp.zeros((8, SEG), F32)
                 for part in range(SEG // 16):
                     at = slice(part * 16, part * 16 + 16)
-                    o = [pcol[c, j, at, :] - rows[c] for c in range(3)]
-                    depth = dot3(o, down)
-                    reach = depth * depth - dot3(o, o)
+                    depth = both[at, k * 2 * SEG : (k * 2 + 1) * SEG]
+                    far = both[at, (k * 2 + 1) * SEG : (k * 2 + 2) * SEG]
                     weight = (
-                        jnp.maximum(depth, 0.0) * jnp.exp2(reach * EXP2_SCALE) * mcol[k, j, at, :]
+                        jnp.maximum(depth, 0.0) * jnp.exp2(depth * depth - far) * mcol[k, j, at, :]
                     )
                     total = total + weight[:8] + weight[8:]
                     top, low = halves(weight)
@@ -503,11 +549,15 @@
         odd = (wtop_b, wlow_b, normals_b)
 
         def contact_pair(half, carry):
+            quadratics(2 * half + 1, pairs_b)
             push(jnp.maximum(2 * half - 1, 0), *odd)
-            contact(2 * half, *even)
+            contact(2 * half, pairs_a, *even)
+            quadratics(jnp.minimum(2 * half + 2, own_rows - 1), pairs_a)
             push(2 * half, *even)
-            contact(2 * half + 1, *odd)
+            contact(2 * half + 1, pairs_b, *odd)
             return carry
+
+        quadratics(0, pairs_a)
 
         lax.fori_loop(0, own_rows // 2, contact_pair, 0)
         push(own_rows - 1, *odd)
@@ -559,11 +609,36 @@
         for c in range(3):
             f_send_m[step, c] = force[3 + c][:GHOST_ROWS]
             f_send_s[step, c] = force[3 + c][GHOST_ROWS:]
-        back_copies = force_copies(step)
+            part[c] = force[c] + slave[c]
+        shared = take(part, own_rows, sids[...])
+        for c in range(3):
+            o_send_m[step, c] = shared[c][:GHOST_ROWS]
+            o_send_s[step, c] = shared[c][GHOST_ROWS:]
+        back_copies = step_copies(step)
         for copy in back_copies:
             copy.start()
         for copy in back_copies:
             copy.wait()
+
+        def ghost_sum(values, hot, from_mesh, from_sub):
+            for c in range(3):
+                for r in range(GHOST_ROWS):
+                    values[c : c + 1, r * SEG : (r + 1) * SEG] = from_mesh[step, c, r : r + 1]
+                    at = (GHOST_ROWS + r) * SEG
+                    values[c : c + 1, at : at + SEG] = from_sub[step, c, r : r + 1]
+            top = values[...].astype(BF16).astype(F32)
+            both = jnp.concatenate([top, values[...] - top], axis=0).astype(BF16)
+            total = dot_nt(both, hot[...])
+            return total[:8] + total[8:]
+
+        sum_m = ghost_sum(values_m, same_m, f_send_m, x_recv_s)
+        sum_s = ghost_sum(values_s, same_s, x_recv_m, f_send_s)
+        for c in range(3):
+            rows = [sum_m[c : c + 1, r * SEG : (r + 1) * SEG] for r in range(GHOST_ROWS)]
+            rows += [sum_s[c : c + 1, r * SEG : (r + 1) * SEG] for r in range(GHOST_ROWS)]
+            owned = jnp.concatenate([o_recv_m[step, c], o_recv_s[step, c]], axis=0)
+            total = owned + jnp.concatenate(rows, axis=0)
+            vel[c, own_rows:, :] = vel[c, own_rows:, :] + TIME_STEP * total / ghost_mass
         terms = []
         for c in range(3):
             came = jnp.concatenate([f_recv_m[step, c], f_recv_s[step, c]], axis=0)
@@ -577,19 +652,12 @@
             terms.append(jnp.concatenate(lows, axis=1))
         added = dot_nt(jnp.concatenate(terms, axis=0), onehot_back[...])
         for c in range(3):
-            own = force[c]
-            own = own + added[c * 32 : c * 32 + own_rows] + added[c * 32 + 16 : c * 32 + 16 + own_rows]
-            now = vel[c, :own_rows, :] + TIME_STEP * (own + slave[c]) / mass[...]
+            own = part[c] + added[c * 32 : c * 32 + own_rows] + added[c * 32 + 16 : c * 32 + 16 + own_rows]
+            now = vel[c, :own_rows, :] + TIME_STEP * own / mass[0]
             vel[c, :own_rows, :] = now
             pos[c] = pos[c] + TIME_STEP * now
         whole.wait_send()
         back.wait_send()
-
-        @pl.when(step < STEPS - 1)
-        def _():
-            stage_velocity(step + 1)
-            for copy in velocity_copies(step + 1):
-                copy.start()
 
         return step_carry
 
@@ -620,7 +688,6 @@
     slots = send_pick.shape[1]
     pairs = cands * own_rows
     table_rows = own_rows + 2 * GHOST_ROWS
-    ghost = (3, GHOST_ROWS, SEG)
     in_vmem = pl.BlockSpec(memory_space=pltpu.VMEM)
     in_smem = pl.BlockSpec(memory_space=pltpu.SMEM)
     v = pltpu.VMEM
@@ -637,7 +704,7 @@
             v((2 * GHOST_ROWS, SEG), jnp.int32),
             v((3, own_rows, SEG), F32),
             v((3, table_rows, SEG), F32),
-            v((own_rows, SEG), F32),
+            v((1, own_rows, SEG), F32),
             v((4, 3, blocks, SEG), F32),
             v((4, 3, blocks, SEG), F32),
             v((3, blocks, SEG), F32),
@@ -649,12 +716,14 @@
             v((SEG, 4 * elems), BF16),
             v((SEG, 2 * GHOST_ROWS * SEG), BF16),
             v((32, 4 * elems), BF16),
-            v((144, 32 * SEG), BF16),
+            *[v((144, 32 * SEG), BF16)] * 2,
             v((4, 3, blocks, SEG), F32),
             v((4, 3, blocks, SEG), F32),
             v((3, table_rows, SEG), F32),
-            v((3, own_rows, SEG, SEG), F32),
+            v((own_rows, SEG, 48), BF16),
             v((cands, own_rows, SEG, SEG), F32),
+            v((SEG, cands * 2 * SEG), F32),
+            v((SEG, cands * 2 * SEG), F32),
             v((SEG, cands * SEG), BF16),
             v((SEG, cands * SEG), BF16),
             v((16, cands * SEG), BF16),
@@ -666,19 +735,13 @@
             v((3, own_rows, SEG), F32),
             v((STEPS, peers, CAP, SEG), F32),
             v((STEPS, peers, CAP, SEG), F32),
-            v(ghost, F32),
-            v(ghost, F32),
-            v(ghost, F32),
-            v(ghost, F32),
-            v((STEPS,) + ghost, F32),
-            v((STEPS,) + ghost, F32),
-            v((STEPS,) + ghost, F32),
-            v((STEPS,) + ghost, F32),
-            v((STEPS,) + ghost, F32),
-            v((STEPS,) + ghost, F32),
-            v((STEPS,) + ghost, F32),
-            v((STEPS,) + ghost, F32),
-            pltpu.SemaphoreType.DMA((4 + STEPS * 8,)),
+            *[v((7, GHOST_ROWS, SEG), F32)] * 4,
+            *[v((2 * GHOST_ROWS, SEG), jnp.int32)] * 2,
+            *[v((GHOST_ROWS * SEG, 2 * GHOST_ROWS * SEG), BF16)] * 2,
+            *[v((8, 2 * GHOST_ROWS * SEG), F32)] * 2,
+            v((3, own_rows, SEG), F32),
+            *[v((STEPS, 3, GHOST_ROWS, SEG), F32)] * 10,
+            pltpu.SemaphoreType.DMA((8 + STEPS * 12,)),
             pltpu.SemaphoreType.DMA((2, STEPS)),
             pltpu.SemaphoreType.DMA((2, STEPS)),
         ],

time: 152 us -> 144 us (0.947)
  Pallas kernels: 149 us -> 141 us
    pallas_call x1, Pallas kernels: 149 us -> 141 us  [per_device(): pl.pallas_call(functools.partial(kernel, own_rows, blocks, cands), out_sh...]
where the time goes in v3:
time: 144 us
  Pallas kernels  141 us (98%)
  local copies, waits for them, and re-layouts  2.04 us (1%)
    pallas_call x1, Pallas kernels, per_device(): pl.pallas_call(functools.partial(kernel, own_rows, blocks, cands), out_sh...  141 us

profile of v3, /device:TPU:1, one launch (start us, length us, event | category | flops | bytes accessed | tf_op | source)
XLA Modules:
  0.0 143.8 jit_solution(8728853575283803886)
XLA Ops:
  0.6 141.1 %shard_map.113 = (f32[3,2048]{1,0:T(4,128)}, f32[3,4096]{1,0:T(4,128)}) custom-call(f32[3,2048]{1,0:T(4,128)} %coords.1, f32[3,2048]{1,0:T(4,128)} %veloc.1, f32[1,2048]{1,0:T(1,128)} %bitcast.3, f32[3,4096]{1,0:T(4,128)} %stress_in.1, s32[4,4096]{1,0:T(4,128)} %connect.1, s32[1,512]{1,0:T(1,128)} %bitcast.4, s32[1,512]{1,0:T(1,128)} %bitcast.5, ...), custom_call_target="tpu_custom_call" | custom-call | tf_op jit(solution)/shard_map/pallas_call | solution.py:694
  141.7 0.0 copy-start
  141.7 1.4 copy.14
  143.1 0.0 copy-done
  143.1 0.6 copy.15
Async XLA Ops:
  141.7 1.4 copy-start

commit v4 on v3

--- a/solution.py
+++ b/solution.py
@@ -155,19 +155,19 @@
         return ring // 2 + (turn + 1) // 2 * (1 - 2 * (turn % 2))
 
     def each_partner(act):
-        def one_z(turn, carry):
-            z = lax.rem(my_z + spread_out(ring_z, turn), ring_z)
-            for turn_x in range(ring_x):
-                x = lax.rem(my_x + spread_out(ring_x, turn_x), ring_x)
+        def one_x(turn, carry):
+            x = lax.rem(my_x + spread_out(ring_x, turn), ring_x)
+            for turn_z in range(ring_z):
+                z = lax.rem(my_z + spread_out(ring_z, turn_z), ring_z)
                 chip = (x * ring_z + z) * 2
                 act(chip + 1 - my_core)
-                if turn_x < ring_x - 1:
+                if turn_z < ring_z - 1:
                     act(chip + my_core)
                 else:
-                    pl.when(turn < ring_z - 1)(lambda chip=chip: act(chip + my_core))
+                    pl.when(turn < ring_x - 1)(lambda chip=chip: act(chip + my_core))
             return carry
 
-        lax.fori_loop(0, ring_z, one_z, 0)
+        lax.fori_loop(0, ring_x, one_x, 0)
 
     barrier = pltpu.get_barrier_semaphore()
 
@@ -609,13 +609,16 @@
         for c in range(3):
             f_send_m[step, c] = force[3 + c][:GHOST_ROWS]
             f_send_s[step, c] = force[3 + c][GHOST_ROWS:]
+        back_copies = step_copies(step)
+        for copy in back_copies[:4]:
+            copy.start()
+        for c in range(3):
             part[c] = force[c] + slave[c]
         shared = take(part, own_rows, sids[...])
         for c in range(3):
             o_send_m[step, c] = shared[c][:GHOST_ROWS]
             o_send_s[step, c] = shared[c][GHOST_ROWS:]
-        back_copies = step_copies(step)
-        for copy in back_copies:
+        for copy in back_copies[4:]:
             copy.start()
         for copy in back_copies:
             copy.wait()

time: 144 us -> 142 us (0.986)
  Pallas kernels: 141 us -> 139 us
    pallas_call x1, Pallas kernels: 141 us -> 139 us  [per_device(): pl.pallas_call(functools.partial(kernel, own_rows, blocks, cands), out_sh...]
where the time goes in v4:
time: 142 us
  Pallas kernels  139 us (98%)
  local copies, waits for them, and re-layouts  2.04 us (1%)
    pallas_call x1, Pallas kernels, per_device(): pl.pallas_call(functools.partial(kernel, own_rows, blocks, cands), out_sh...  139 us

profile of v4, /device:TPU:1, one launch (start us, length us, event | category | flops | bytes accessed | tf_op | source)
XLA Modules:
  0.0 142.1 jit_solution(9170571149085326386)
XLA Ops:
  0.6 139.4 %shard_map.113 = (f32[3,2048]{1,0:T(4,128)}, f32[3,4096]{1,0:T(4,128)}) custom-call(f32[3,2048]{1,0:T(4,128)} %coords.1, f32[3,2048]{1,0:T(4,128)} %veloc.1, f32[1,2048]{1,0:T(1,128)} %bitcast.3, f32[3,4096]{1,0:T(4,128)} %stress_in.1, s32[4,4096]{1,0:T(4,128)} %connect.1, s32[1,512]{1,0:T(1,128)} %bitcast.4, s32[1,512]{1,0:T(1,128)} %bitcast.5, ...), custom_call_target="tpu_custom_call" | custom-call | tf_op jit(solution)/shard_map/pallas_call | solution.py:697
  140.0 0.0 copy-start
  140.0 1.4 copy.14
  141.4 0.0 copy-done
  141.4 0.6 copy.15
Async XLA Ops:
  140.0 1.4 %copy-start = (f32[3,4096]{1,0:T(4,128)S(1)}, f32[3,4096]{1,0:T(4,128)}, u32[]{:S(2)}) copy-start(f32[3,4096]{1,0:T(4,128)} %get-tuple-element.5) | copy-start | bytes 147460

commit v5 on v4

--- a/solution.py
+++ b/solution.py
@@ -610,17 +610,23 @@
             f_send_m[step, c] = force[3 + c][:GHOST_ROWS]
             f_send_s[step, c] = force[3 + c][GHOST_ROWS:]
         back_copies = step_copies(step)
-        for copy in back_copies[:4]:
+        for copy in back_copies[2:4]:
             copy.start()
         for c in range(3):
             part[c] = force[c] + slave[c]
-        shared = take(part, own_rows, sids[...])
-        for c in range(3):
-            o_send_m[step, c] = shared[c][:GHOST_ROWS]
-            o_send_s[step, c] = shared[c][GHOST_ROWS:]
-        for copy in back_copies[4:]:
-            copy.start()
-        for copy in back_copies:
+
+        @pl.when(step < STEPS - 1)
+        def _():
+            for copy in back_copies[:2]:
+                copy.start()
+            shared = take(part, own_rows, sids[...])
+            for c in range(3):
+                o_send_m[step, c] = shared[c][:GHOST_ROWS]
+                o_send_s[step, c] = shared[c][GHOST_ROWS:]
+            for copy in back_copies[4:]:
+                copy.start()
+
+        for copy in back_copies[2:4]:
             copy.wait()
 
         def ghost_sum(values, hot, from_mesh, from_sub):
@@ -634,14 +640,19 @@
             total = dot_nt(both, hot[...])
             return total[:8] + total[8:]
 
-        sum_m = ghost_sum(values_m, same_m, f_send_m, x_recv_s)
-        sum_s = ghost_sum(values_s, same_s, x_recv_m, f_send_s)
-        for c in range(3):
-            rows = [sum_m[c : c + 1, r * SEG : (r + 1) * SEG] for r in range(GHOST_ROWS)]
-            rows += [sum_s[c : c + 1, r * SEG : (r + 1) * SEG] for r in range(GHOST_ROWS)]
-            owned = jnp.concatenate([o_recv_m[step, c], o_recv_s[step, c]], axis=0)
-            total = owned + jnp.concatenate(rows, axis=0)
-            vel[c, own_rows:, :] = vel[c, own_rows:, :] + TIME_STEP * total / ghost_mass
+        @pl.when(step < STEPS - 1)
+        def _():
+            for copy in back_copies[:2] + back_copies[4:]:
+                copy.wait()
+            sum_m = ghost_sum(values_m, same_m, f_send_m, x_recv_s)
+            sum_s = ghost_sum(values_s, same_s, x_recv_m, f_send_s)
+            for c in range(3):
+                rows = [sum_m[c : c + 1, r * SEG : (r + 1) * SEG] for r in range(GHOST_ROWS)]
+                rows += [sum_s[c : c + 1, r * SEG : (r + 1) * SEG] for r in range(GHOST_ROWS)]
+                owned = jnp.concatenate([o_recv_m[step, c], o_recv_s[step, c]], axis=0)
+                total = owned + jnp.concatenate(rows, axis=0)
+                vel[c, own_rows:, :] = vel[c, own_rows:, :] + TIME_STEP * total / ghost_mass
+
         terms = []
         for c in range(3):
             came = jnp.concatenate([f_recv_m[step, c], f_recv_s[step, c]], axis=0)

time: 142 us -> 141 us (level)
  no operation moved by 1% of the time
where the time goes in v5:
time: 141 us
  Pallas kernels  138 us (98%)
  local copies, waits for them, and re-layouts  2.04 us (1%)
    pallas_call x1, Pallas kernels, per_device(): pl.pallas_call(functools.partial(kernel, own_rows, blocks, cands), out_sh...  138 us

profile of v5, /device:TPU:1, one launch (start us, length us, event | category | flops | bytes accessed | tf_op | source)
XLA Modules:
  0.0 141.1 jit_solution(18109777715413922890)
XLA Ops:
  0.6 138.4 %shard_map.113 = (f32[3,2048]{1,0:T(4,128)}, f32[3,4096]{1,0:T(4,128)}) custom-call(f32[3,2048]{1,0:T(4,128)} %coords.1, f32[3,2048]{1,0:T(4,128)} %veloc.1, f32[1,2048]{1,0:T(1,128)} %bitcast.3, f32[3,4096]{1,0:T(4,128)} %stress_in.1, s32[4,4096]{1,0:T(4,128)} %connect.1, s32[1,512]{1,0:T(1,128)} %bitcast.4, s32[1,512]{1,0:T(1,128)} %bitcast.5, ...), custom_call_target="tpu_custom_call" | custom-call | tf_op jit(solution)/shard_map/pallas_call | solution.py:708
  139.0 0.0 copy-start
  139.0 1.4 copy.14
  140.4 0.0 copy-done
  140.4 0.6 copy.15
Async XLA Ops:
  139.0 1.4 %copy-start = (f32[3,4096]{1,0:T(4,128)S(1)}, f32[3,4096]{1,0:T(4,128)}, u32[]{:S(2)}) copy-start(f32[3,4096]{1,0:T(4,128)} %get-tuple-element.5) | copy-start | bytes 147460
